TPU v7x, 256 devices: a whole 4x4x8 slice. The times are simulated.
256 devices in a mesh: seq: 64 (over z, y, core), fsdp: 4 (over x).
Axes of the slice: x: 4, y: 4, z: 8, core: 2. Of those that a mesh axis runs over, the one named last changes fastest.
Arguments:
- inputs: bfloat16 [4, 8192, 3584], P('fsdp', 'seq'), may hold values from -36 to 36
- keys_queries: bfloat16 [4, 8192, 256], P('fsdp', 'seq'), may hold values from -0.29882812 to 0.29882812
- log_decay: float32 [4, 56, 8192], P('fsdp', None, 'seq'), may hold values from -1.5 to 0, as said below
- skip: float32 [56], replicated, may hold values from 0.5 to 1.5
- classifier: bfloat16 [3584, 128], P('fsdp'), may hold values from -0.09375 to 0.09375
Outputs:
- mixed: bfloat16 [4, 8192, 3584], P('fsdp', 'seq')
- logits: float32 [4, 128], P('fsdp')
Inputs may be any that keep to these rules, and one draw needn't show every extreme that they name: `log_decay`: log-decays are negative.
All inputs are finite; a program needn't handle non-finite values.
Results may differ from a plain program's by a relative error of at most 0.0051.
Values may be sent and summed in bfloat16 or wider, within the bound.
A program may use at most 256 MiB of HBM per device.

v0:
```python
import jax
import jax.numpy as jnp
from jax import lax
from jax.sharding import PartitionSpec as P

N = 128
GROUP = 128
epsilon = 1e-06


def linker(earlier, latter):
    return (earlier[0] + latter[0], jnp.exp(latter[0]) * earlier[1] + latter[1])


def local(inputs, keys_queries, log_decay, skip, classifier):
    copies, positions, channels = inputs.shape
    head_count = log_decay.shape[1]
    head_dim = channels // head_count
    blocks = positions // GROUP
    key_rows = keys_queries[:, :, :N].reshape(copies, blocks, GROUP, N)
    queries = keys_queries[:, :, N:].reshape(copies, blocks, GROUP, N)
    values = inputs.reshape(copies, blocks, GROUP, head_count, head_dim)
    cumulative = jnp.cumsum(log_decay.reshape(copies, head_count, blocks, GROUP), axis=-1)
    block_decay = cumulative[..., -1]
    weighted = (key_rows[:, None] * jnp.exp(block_decay[..., None] - cumulative)[..., None]).astype(
        jnp.bfloat16
    )
    block_state = jnp.einsum(
        "chkun,ckuhp->kchnp", weighted, values, preferred_element_type=jnp.float32
    )

    def advance(running, member):
        return (jnp.exp(member[0])[..., None, None] * running + member[1], running)

    device_state, starts = lax.scan(
        advance, jnp.zeros_like(block_state[0]), (jnp.moveaxis(block_decay, 2, 0), block_state)
    )
    device_decay = jnp.sum(block_decay, axis=-1)
    axis_count = lax.axis_size("seq")
    flattened = device_state.reshape(copies, head_count, 1, N * head_dim)
    decay_copies = jnp.broadcast_to(
        device_decay[:, :, None, None], (copies, head_count, 1, axis_count)
    )
    totals = lax.associative_scan(
        linker,
        (
            lax.all_to_all(decay_copies, "seq", split_axis=3, concat_axis=2, tiled=True),
            lax.all_to_all(flattened, "seq", split_axis=3, concat_axis=2, tiled=True),
        ),
        axis=2,
    )[1]
    shifted = jnp.concatenate([jnp.zeros_like(totals[:, :, :1]), totals[:, :, :-1]], axis=2)
    incoming = lax.all_to_all(shifted, "seq", split_axis=2, concat_axis=3, tiled=True)
    incoming = incoming.reshape(copies, head_count, N, head_dim)
    preceding = jnp.moveaxis(jnp.cumsum(block_decay, axis=-1) - block_decay, 2, 0)
    carried = (jnp.exp(preceding)[..., None, None] * incoming[None] + starts).astype(jnp.bfloat16)
    growth = jnp.exp(cumulative).transpose(0, 2, 3, 1)[..., None]
    carried_out = (
        jnp.einsum("ckqn,kchnp->ckqhp", queries, carried, preferred_element_type=jnp.float32)
        * growth
    )
    causal = jnp.arange(GROUP)[:, None] >= jnp.arange(GROUP)[None, :]
    scores = jnp.einsum("cktn,ckun->cktu", queries, key_rows, preferred_element_type=jnp.float32)
    decay_gap = jnp.where(causal, cumulative[..., :, None] - cumulative[..., None, :], -jnp.inf)
    mixing = (scores[:, None] * jnp.exp(decay_gap)).astype(jnp.bfloat16)
    diagonal = jnp.einsum("chktu,ckuhp->ckthp", mixing, values, preferred_element_type=jnp.float32)
    mixed_full = diagonal + carried_out + skip[:, None] * values.astype(jnp.float32)
    mixed = mixed_full.astype(jnp.bfloat16).reshape(copies, positions, channels)
    partial_sum = jnp.sum(mixed_full, axis=(1, 2)).reshape(copies, channels)
    pooled = lax.psum(partial_sum, "seq") / (positions * lax.axis_size("seq"))
    normed = (
        pooled / jnp.sqrt(jnp.mean(pooled * pooled, axis=-1, keepdims=True) + epsilon)
    ).astype(jnp.bfloat16)
    logits = jnp.dot(
        normed,
        lax.all_gather(classifier, "fsdp", axis=0, tiled=True),
        preferred_element_type=jnp.float32,
    )
    return (mixed, logits)


def solution(mesh):
    return jax.shard_map(
        local,
        mesh=mesh,
        in_specs=(
            P("fsdp", "seq", None),
            P("fsdp", "seq", None),
            P("fsdp", None, "seq"),
            P(),
            P("fsdp", None),
        ),
        out_specs=(P("fsdp", "seq", None), P("fsdp", None)),
        check_vma=False,
    )
```

profile of v0, /device:TPU:2, one launch (start us, length us, event | category | flops | bytes accessed | tf_op | source)
XLA Modules:
  0.0 497.6 jit_solution(18033312582586399048)
XLA Ops:
  2.5 12.1 %all-to-all-start.1 = ((f32[1,56,1,64]{1,2,0,3:T(1,128)}), f32[1,56,1,64]{1,2,0,3:T(1,128)S(1)}, u32[]{:S(2)}, u32[]{:S(2)}) async-start(f32[1,56,1,64]{1,2,0,3:T(1,128)} %broadcast_in_dim.18), calls=%async_computation.1 | async-start | bytes 65536 | tf_op jit(solution)/shard_map/all_to_all | solution.py:47
  14.7 1.6 copy.45
  17.6 4.5 copy.57
  22.6 38.4 %reduce.6 = f32[8192,56]{1,0:T(8,128)} reduce(f32[8192,1,1,56]{3,2,1,0:T(1,128)} %bitcast.76, f32[]{:T(128)} %broadcast.116), dimensions={1,2}, to_apply=%bitcast.65.reduce_sub_computation | reduce | bytes 3670020
  61.0 6.9 %reshape.245 = f32[64,1,7168]{2,1,0:T(1,128)} reshape(f32[8192,56]{1,0:T(8,128)} %reduce.6) | data formatting | bytes 3670016
  67.9 10.5 %all-to-all-start = ((f32[64,1,7168]{2,1,0:T(1,128)}), f32[64,1,7168]{2,1,0:T(1,128)S(1)}, u32[]{:S(2)}, u32[]{:S(2)}) async-start(f32[64,1,7168]{2,1,0:T(1,128)} %reshape.245), calls=%async_computation | async-start | bytes 3670016 | tf_op jit(solution)/shard_map/all_to_all | solution.py:48
  78.8 45.2 %all-to-all-done = f32[64,1,7168]{2,1,0:T(1,128)S(1)} async-done(((f32[64,1,7168]{2,1,0:T(1,128)}), f32[64,1,7168]{2,1,0:T(1,128)S(1)}, u32[]{:S(2)}, u32[]{:S(2)}) %all-to-all-start) | async-done | bytes 1835040 | tf_op jit(solution)/shard_map/all_to_all | solution.py:48
  124.0 6.8 %reduce.7 = f32[64,7168]{1,0:T(8,128)} reduce(f32[64,1,7168]{2,1,0:T(1,128)S(1)} %all-to-all-done, f32[]{:T(128)} %broadcast.116), dimensions={1}, to_apply=%all_to_all.10.reduce_sub_computation | reduce | bytes 3670020 | tf_op jit(solution)/shard_map/all_to_all | solution.py:48
  130.7 11.1 %reshape.246 = f32[8192,1,1,56]{3,2,1,0:T(1,128)} reshape(f32[64,7168]{1,0:T(8,128)} %reduce.7) | data formatting | bytes 3670016
  141.8 4.1 fusion.34
  148.0 2.2 copy.60
  157.4 16.4 %pad.85 = f32[1,56,64,128]{3,1,0,2:T(8,128)} pad(f32[1,56,32,128]{3,1,0,2:T(8,128)} %add.138, f32[]{:T(128)} %constant.16.clone.1), padding=0_0_0x0_0_0x1_0_1x0_0_0 | pad | bytes 2752516
  173.8 1.5 copy.62
  175.4 1.8 fusion.11
  177.2 11.0 %pad.61 = f32[1,56,63,128]{3,1,0,2:T(8,128)} pad(f32[1,56,32,128]{3,1,0,2:T(8,128)S(1)} %pad_maximum_fusion, f32[]{:T(128)} %constant.16.clone.1), padding=0_0_0x0_0_0x0_0_1x0_0_0 | pad | bytes 2723844 | tf_op jit(solution)/shard_map/slice | solution.py:52
  188.3 1.7 slice_add_fusion.5
  191.3 5.3 %all-to-all-start.2 = ((f32[1,56,64,128]{3,1,0,2:T(8,128)}), f32[1,56,64,128]{3,1,0,2:T(8,128)S(1)}, u32[]{:S(2)}, u32[]{:S(2)}) async-start(f32[1,56,64,128]{3,1,0,2:T(8,128)} %concatenate.23), calls=%async_computation.2 | async-start | bytes 3670016 | tf_op jit(solution)/shard_map/all_to_all | solution.py:53
  196.6 2.6 copy.54
  199.4 2.6 fusion
  202.0 15.5 %all_gather.3 = bf16[3584,128]{1,0:T(8,128)(2,1)} all-gather(bf16[896,128]{1,0:T(8,128)(2,1)S(1)} %copy-done.10), channel_id=1, replica_groups=mesh['seq'=64,'fsdp'=4] {'fsdp'}, dimensions={0}, use_global_device_ids=true | all-gather | bytes 1146880 | tf_op jit(solution)/shard_map/all_gather | solution.py:76
  217.5 24.9 %all-to-all-done.2 = f32[1,56,64,128]{3,1,0,2:T(8,128)S(1)} async-done(((f32[1,56,64,128]{3,1,0,2:T(8,128)}), f32[1,56,64,128]{3,1,0,2:T(8,128)S(1)}, u32[]{:S(2)}, u32[]{:S(2)}) %all-to-all-start.2) | async-done | bytes 1835040 | tf_op jit(solution)/shard_map/all_to_all | solution.py:53
  242.8 1.7 convert_element_type.57
  244.6 3.3 fusion.35
  248.0 246.3 %psum.7 = f32[1,3584]{1,0:T(1,128)S(1)} all-reduce(f32[1,3584]{1,0:T(1,128)S(1)} %reshape.236), channel_id=1, replica_groups=mesh['seq'=64,'fsdp'=4] {'seq'}, use_global_device_ids=true, to_apply=%region_2.3 | all-reduce | flops 3584 | bytes 28672 | tf_op jit(solution)/shard_map/psum | solution.py:70
  (103 shorter events, 18.1 us)
Async XLA Ops:
  0.6 15.7 %copy-start.8 = (bf16[1,128,256]{2,1,0:T(8,128)(2,1)S(1)}, bf16[1,128,256]{2,1,0:T(8,128)(2,1)}, u32[]{:S(2)}) copy-start(bf16[1,128,256]{2,1,0:T(8,128)(2,1)} %param.6) | copy-start | bytes 196612
  2.5 65.4 %all-to-all-start.1 = ((f32[1,56,1,64]{1,2,0,3:T(1,128)}), f32[1,56,1,64]{1,2,0,3:T(1,128)S(1)}, u32[]{:S(2)}, u32[]{:S(2)}) async-start(f32[1,56,1,64]{1,2,0,3:T(1,128)} %broadcast_in_dim.18), calls=%async_computation.1 | async-start | bytes 65536 | tf_op jit(solution)/shard_map/all_to_all | solution.py:47
  16.3 5.8 %copy-start.5 = (bf16[1,128,3584]{1,2,0:T(8,128)(2,1)}, bf16[1,128,3584]{1,2,0:T(8,128)(2,1)S(1)}, u32[]{:S(2)}) copy-start(bf16[1,128,3584]{1,2,0:T(8,128)(2,1)S(1)} %copy.45) | copy-start | bytes 2752516
  67.9 56.0 %all-to-all-start = ((f32[64,1,7168]{2,1,0:T(1,128)}), f32[64,1,7168]{2,1,0:T(1,128)S(1)}, u32[]{:S(2)}, u32[]{:S(2)}) async-start(f32[64,1,7168]{2,1,0:T(1,128)} %reshape.245), calls=%async_computation | async-start | bytes 3670016 | tf_op jit(solution)/shard_map/all_to_all | solution.py:48
  141.8 4.1 copy-start
  155.4 0.9 copy-start.2
  157.4 16.4 %copy-start.1 = (f32[1,56,31,128]{1,3,2,0:T(8,128)S(1)}, f32[1,56,31,128]{1,3,2,0:T(8,128)}, u32[]{:S(2)}) copy-start(f32[1,56,31,128]{1,3,2,0:T(8,128)} %slice.192) | copy-start | bytes 2666500
  173.8 1.5 copy-start.9
  177.2 11.1 %copy-start.4 = (f32[1,56,64,128]{3,1,0,2:T(8,128)S(1)}, f32[1,56,64,128]{3,1,0,2:T(8,128)}, u32[]{:S(2)}) copy-start(f32[1,56,64,128]{3,1,0,2:T(8,128)} %pad.85) | copy-start | bytes 5505028
  191.3 51.1 %all-to-all-start.2 = ((f32[1,56,64,128]{3,1,0,2:T(8,128)}), f32[1,56,64,128]{3,1,0,2:T(8,128)S(1)}, u32[]{:S(2)}, u32[]{:S(2)}) async-start(f32[1,56,64,128]{3,1,0,2:T(8,128)} %concatenate.23), calls=%async_computation.2 | async-start | bytes 3670016 | tf_op jit(solution)/shard_map/all_to_all | solution.py:53
  196.6 2.8 copy-start.6
  199.4 2.6 copy-start.10
  242.8 1.8 copy-start.3
  242.8 1.8 copy-start.11
  247.9 249.0 %copy-start.7 = (bf16[3584,128]{1,0:T(8,128)(2,1)S(1)}, bf16[3584,128]{1,0:T(8,128)(2,1)}, u32[]{:S(2)}) copy-start(bf16[3584,128]{1,0:T(8,128)(2,1)} %all_gather.3) | copy-start | bytes 2752516
where the time goes:
time: 500 us; the launch traced here: 498 us
  blocking collectives  262 us (52%)
  local copies, waits for them, and re-layouts  73.5 us (15%)
  waiting for transfers between devices  70.1 us (14%)
  other arithmetic  54.6 us (11%)
  starting transfers between devices  27.9 us (6%)
  matrix products  7.99 us (2%)
    psum x1, blocking collectives, local(): pooled = lax.psum(partial_sum, 'seq') / (positions * lax.axis_size('seq'))  246 us
    all_to_all x1, waiting for transfers between devices, local(): lax.all_to_all(flattened, 'seq', split_axis=3, concat_axis=2, tiled=True)  45.2 us
    unnamed x34, local copies, waits for them, and re-layouts  44 us
    unnamed x1, other arithmetic  38.4 us
    all_to_all x1, waiting for transfers between devices, local(): lax.all_to_all(shifted, 'seq', split_axis=2, concat_axis=3, tiled=True)  24.9 us
    all_gather x1, blocking collectives, local(): lax.all_gather(classifier, 'fsdp', axis=0, tiled=True)  15.5 us
    all_to_all x1, starting transfers between devices, local(): lax.all_to_all(decay_copies, 'seq', split_axis=3, concat_axis=2, tiled=True)  12.1 us
    slice x1, local copies, waits for them, and re-layouts, local(): totals[:, :, :-1]  11 us
  transfers between devices with their start and end apart: 3, of which 2 were waited for; matrix products, arithmetic and copies ran while one was open for 12% of the time, Pallas kernels for 0%

commit v1 on v0

--- a/solution.py
+++ b/solution.py
@@ -67,7 +67,9 @@
     mixed_full = diagonal + carried_out + skip[:, None] * values.astype(jnp.float32)
     mixed = mixed_full.astype(jnp.bfloat16).reshape(copies, positions, channels)
     partial_sum = jnp.sum(mixed_full, axis=(1, 2)).reshape(copies, channels)
-    pooled = lax.psum(partial_sum, "seq") / (positions * lax.axis_size("seq"))
+    pooled = jnp.sum(lax.all_gather(partial_sum, "seq"), axis=0) / (
+        positions * lax.axis_size("seq")
+    )
     normed = (
         pooled / jnp.sqrt(jnp.mean(pooled * pooled, axis=-1, keepdims=True) + epsilon)
     ).astype(jnp.bfloat16)

time: 500 us -> 306 us (0.61)
  blocking collectives: 262 us -> 65.6 us
    psum x1 -> x0, blocking collectives: 246 us -> none  [local(): pooled = lax.psum(partial_sum, 'seq') / (positions * lax.axis_size('seq'))]
    all_gather x0 -> x1, blocking collectives: none -> 50.2 us  [local(): lax.all_gather(partial_sum, 'seq')]
  transfers between devices with their start and end apart: 3 -> 3, of which waited for: 2 -> 2; matrix products, arithmetic and copies ran while one was open for 12% -> 19% of each run, Pallas kernels for 0% -> 0%
where the time goes in v1:
time: 306 us; the launch traced here: 302 us
  local copies, waits for them, and re-layouts  73.5 us (24%)
  waiting for transfers between devices  70.1 us (23%)
  blocking collectives  65.6 us (21%)
  other arithmetic  55.1 us (18%)
  starting transfers between devices  27.9 us (9%)
  matrix products  7.99 us (3%)
    all_gather x1, blocking collectives, local(): lax.all_gather(partial_sum, 'seq')  50.2 us
    all_to_all x1, waiting for transfers between devices, local(): lax.all_to_all(flattened, 'seq', split_axis=3, concat_axis=2, tiled=True)  45.2 us
    unnamed x34, local copies, waits for them, and re-layouts  44 us
    unnamed x1, other arithmetic  38.4 us
    all_to_all x1, waiting for transfers between devices, local(): lax.all_to_all(shifted, 'seq', split_axis=2, concat_axis=3, tiled=True)  24.9 us
    all_gather x1, blocking collectives, local(): lax.all_gather(classifier, 'fsdp', axis=0, tiled=True)  15.5 us
    all_to_all x1, starting transfers between devices, local(): lax.all_to_all(decay_copies, 'seq', split_axis=3, concat_axis=2, tiled=True)  12.1 us
    slice x1, local copies, waits for them, and re-layouts, local(): totals[:, :, :-1]  11 us
  transfers between devices with their start and end apart: 3, of which 2 were waited for; matrix products, arithmetic and copies ran while one was open for 19% of the time, Pallas kernels for 0%

profile of v1, /device:TPU:2, one launch (start us, length us, event | category | flops | bytes accessed | tf_op | source)
XLA Modules:
  0.0 302.0 jit_solution(15744556721898108986)
XLA Ops:
  2.5 12.1 %all-to-all-start.1 = ((f32[1,56,1,64]{1,2,0,3:T(1,128)}), f32[1,56,1,64]{1,2,0,3:T(1,128)S(1)}, u32[]{:S(2)}, u32[]{:S(2)}) async-start(f32[1,56,1,64]{1,2,0,3:T(1,128)} %broadcast_in_dim.18), calls=%async_computation.1 | async-start | bytes 65536 | tf_op jit(solution)/shard_map/all_to_all | solution.py:47
  14.7 1.6 copy.34
  17.6 4.5 %copy.46 = f32[56,128,64]{0,2,1:T(8,128)} copy(f32[56,128,64]{1,2,0:T(8,128)S(1)} %fusion.10) | data formatting | bytes 3670016 | tf_op jit(solution)/shard_map/reshape | solution.py:40
  22.6 38.4 %reduce.8 = f32[8192,56]{1,0:T(8,128)} reduce(f32[8192,1,1,56]{3,2,1,0:T(1,128)} %bitcast.74, f32[]{:T(128)} %broadcast.126), dimensions={1,2}, to_apply=%bitcast.62.reduce_sub_computation | reduce | bytes 3670020
  61.0 6.9 %reshape.248 = f32[64,1,7168]{2,1,0:T(1,128)} reshape(f32[8192,56]{1,0:T(8,128)} %reduce.8) | data formatting | bytes 3670016
  67.9 10.5 %all-to-all-start = ((f32[64,1,7168]{2,1,0:T(1,128)}), f32[64,1,7168]{2,1,0:T(1,128)S(1)}, u32[]{:S(2)}, u32[]{:S(2)}) async-start(f32[64,1,7168]{2,1,0:T(1,128)} %reshape.248), calls=%async_computation | async-start | bytes 3670016 | tf_op jit(solution)/shard_map/all_to_all | solution.py:48
  78.8 45.2 %all-to-all-done = f32[64,1,7168]{2,1,0:T(1,128)S(1)} async-done(((f32[64,1,7168]{2,1,0:T(1,128)}), f32[64,1,7168]{2,1,0:T(1,128)S(1)}, u32[]{:S(2)}, u32[]{:S(2)}) %all-to-all-start) | async-done | bytes 1835040 | tf_op jit(solution)/shard_map/all_to_all | solution.py:48
  124.0 6.8 %reduce.9 = f32[64,7168]{1,0:T(8,128)} reduce(f32[64,1,7168]{2,1,0:T(1,128)S(1)} %all-to-all-done, f32[]{:T(128)} %broadcast.126), dimensions={1}, to_apply=%all_to_all.10.reduce_sub_computation | reduce | bytes 3670020 | tf_op jit(solution)/shard_map/all_to_all | solution.py:48
  130.7 11.1 %reshape.249 = f32[8192,1,1,56]{3,2,1,0:T(1,128)} reshape(f32[64,7168]{1,0:T(8,128)} %reduce.9) | data formatting | bytes 3670016
  141.8 4.1 %fusion.26 = (f32[1,56,32,128]{1,3,2,0:T(8,128)}, f32[1,56,32,128]{1,3,2,0:T(8,128)S(1)}) fusion(f32[1,56,64,128]{1,3,2,0:T(8,128)} %bitcast.71), kind=kLoop, calls=%fused_computation.69 | loop fusion | bytes 3670016 | tf_op jit(solution)/shard_map/slice | solution.py:44
  148.0 2.2 copy.49
  157.4 16.4 %pad.85 = f32[1,56,64,128]{3,1,0,2:T(8,128)} pad(f32[1,56,32,128]{3,1,0,2:T(8,128)} %add.136, f32[]{:T(128)} %constant.16.clone.1), padding=0_0_0x0_0_0x1_0_1x0_0_0 | pad | bytes 2752516
  173.8 1.5 copy.51
  175.4 1.8 fusion.11
  177.2 11.0 %pad.61 = f32[1,56,63,128]{3,1,0,2:T(8,128)} pad(f32[1,56,32,128]{3,1,0,2:T(8,128)S(1)} %pad_maximum_fusion, f32[]{:T(128)} %constant.16.clone.1), padding=0_0_0x0_0_0x0_0_1x0_0_0 | pad | bytes 2723844 | tf_op jit(solution)/shard_map/slice | solution.py:52
  188.3 1.7 slice_add_fusion.5
  191.3 5.3 %all-to-all-start.2 = ((f32[1,56,64,128]{3,1,0,2:T(8,128)}), f32[1,56,64,128]{3,1,0,2:T(8,128)S(1)}, u32[]{:S(2)}, u32[]{:S(2)}) async-start(f32[1,56,64,128]{3,1,0,2:T(8,128)} %concatenate.23), calls=%async_computation.2 | async-start | bytes 3670016 | tf_op jit(solution)/shard_map/all_to_all | solution.py:53
  196.6 2.6 copy.43
  199.4 2.6 fusion
  202.0 15.5 %all_gather.7 = bf16[3584,128]{1,0:T(8,128)(2,1)} all-gather(bf16[896,128]{1,0:T(8,128)(2,1)S(1)} %copy-done.10), channel_id=1, replica_groups=mesh['seq'=64,'fsdp'=4] {'fsdp'}, dimensions={0}, use_global_device_ids=true | all-gather | bytes 1146880 | tf_op jit(solution)/shard_map/all_gather | solution.py:78
  217.5 24.9 %all-to-all-done.2 = f32[1,56,64,128]{3,1,0,2:T(8,128)S(1)} async-done(((f32[1,56,64,128]{3,1,0,2:T(8,128)}), f32[1,56,64,128]{3,1,0,2:T(8,128)S(1)}, u32[]{:S(2)}, u32[]{:S(2)}) %all-to-all-start.2) | async-done | bytes 1835040 | tf_op jit(solution)/shard_map/all_to_all | solution.py:53
  242.8 1.7 convert_element_type.60
  244.6 3.3 %fusion.27 = (f32[56,64]{1,0:T(8,128)S(1)}, bf16[1,1,128,56,64]{2,4,3,1,0:T(8,128)(2,1)S(1)}) fusion(f32[1,1,128,56,64]{2,4,3,1,0:T(8,128)S(1)} %bitcast.75, f32[56]{0:T(128)S(1)} %copy-done.11, f32[128,56]{0,1:T(8,128)S(1)} %exponential_bitcast_fusion, bf16[56,128,64]{2,1,0:T(8,128)(2,1)} %convert_element_type.60, bf16[1,128,256]{2,1,0:T(8,128)(2,1)S(1)} %copy-done.8, ...), kind=kOutput, calls=%fused_computation.70 | convolution fusion | flops 120189440 | bytes 5581312 | tf_op jit(solution)/shard_map/ckqn,kchnp->ckqhp/dot_general | solution.py:59
  248.0 50.2 %all_gather.6 = f32[64,1,3584]{2,1,0:T(1,128)S(1)} all-gather(f32[1,1,3584]{2,1,0:T(1,128)S(1)} %all_gather_reshape.3), channel_id=1, replica_groups=mesh['seq'=64,'fsdp'=4] {'seq'}, dimensions={0}, use_global_device_ids=true | all-gather | bytes 931840 | tf_op jit(solution)/shard_map/all_gather | solution.py:70
  (106 shorter events, 18.6 us)
Async XLA Ops:
  0.6 15.7 %copy-start.8 = (bf16[1,128,256]{2,1,0:T(8,128)(2,1)S(1)}, bf16[1,128,256]{2,1,0:T(8,128)(2,1)}, u32[]{:S(2)}) copy-start(bf16[1,128,256]{2,1,0:T(8,128)(2,1)} %param.6) | copy-start | bytes 196612
  2.5 65.4 %all-to-all-start.1 = ((f32[1,56,1,64]{1,2,0,3:T(1,128)}), f32[1,56,1,64]{1,2,0,3:T(1,128)S(1)}, u32[]{:S(2)}, u32[]{:S(2)}) async-start(f32[1,56,1,64]{1,2,0,3:T(1,128)} %broadcast_in_dim.18), calls=%async_computation.1 | async-start | bytes 65536 | tf_op jit(solution)/shard_map/all_to_all | solution.py:47
  16.3 5.8 %copy-start.5 = (bf16[1,128,3584]{1,2,0:T(8,128)(2,1)}, bf16[1,128,3584]{1,2,0:T(8,128)(2,1)S(1)}, u32[]{:S(2)}) copy-start(bf16[1,128,3584]{1,2,0:T(8,128)(2,1)S(1)} %copy.34) | copy-start | bytes 2752516
  67.9 56.0 %all-to-all-start = ((f32[64,1,7168]{2,1,0:T(1,128)}), f32[64,1,7168]{2,1,0:T(1,128)S(1)}, u32[]{:S(2)}, u32[]{:S(2)}) async-start(f32[64,1,7168]{2,1,0:T(1,128)} %reshape.248), calls=%async_computation | async-start | bytes 3670016 | tf_op jit(solution)/shard_map/all_to_all | solution.py:48
  141.8 4.1 %copy-start = (f32[8192,1,1,56]{3,2,1,0:T(1,128)S(1)}, f32[8192,1,1,56]{3,2,1,0:T(1,128)}, u32[]{:S(2)}) copy-start(f32[8192,1,1,56]{3,2,1,0:T(1,128)} %reshape.249) | copy-start | bytes 5505028
  155.4 0.9 copy-start.2
  157.4 16.4 %copy-start.1 = (f32[1,56,31,128]{1,3,2,0:T(8,128)S(1)}, f32[1,56,31,128]{1,3,2,0:T(8,128)}, u32[]{:S(2)}) copy-start(f32[1,56,31,128]{1,3,2,0:T(8,128)} %slice.192) | copy-start | bytes 2666500
  173.8 1.5 copy-start.9
  177.2 11.1 %copy-start.4 = (f32[1,56,64,128]{3,1,0,2:T(8,128)S(1)}, f32[1,56,64,128]{3,1,0,2:T(8,128)}, u32[]{:S(2)}) copy-start(f32[1,56,64,128]{3,1,0,2:T(8,128)} %pad.85) | copy-start | bytes 5505028
  191.3 51.1 %all-to-all-start.2 = ((f32[1,56,64,128]{3,1,0,2:T(8,128)}), f32[1,56,64,128]{3,1,0,2:T(8,128)S(1)}, u32[]{:S(2)}, u32[]{:S(2)}) async-start(f32[1,56,64,128]{3,1,0,2:T(8,128)} %concatenate.23), calls=%async_computation.2 | async-start | bytes 3670016 | tf_op jit(solution)/shard_map/all_to_all | solution.py:53
  196.6 2.8 copy-start.6
  199.4 2.6 copy-start.10
  242.8 1.8 copy-start.3
  242.8 1.8 copy-start.11
  248.0 53.3 %copy-start.7 = (bf16[3584,128]{1,0:T(8,128)(2,1)S(1)}, bf16[3584,128]{1,0:T(8,128)(2,1)}, u32[]{:S(2)}) copy-start(bf16[3584,128]{1,0:T(8,128)(2,1)} %all_gather.7) | copy-start | bytes 2752516
